TPU v7x, 32 devices: a whole 2x2x4 slice. The times are simulated.
32 devices in a mesh: dp: 8 (over z, y), tensor: 4 (over x, core).
Axes of the slice: x: 2, y: 2, z: 4, core: 2. Of those that a mesh axis runs over, the one named last changes fastest.
Arguments:
- hidden: bfloat16 [128, 4608], P('dp'), may hold values from -6 to 6
- tied_table: bfloat16 [16384, 4608], P(('dp', 'tensor')), may hold values from -0.25 to 0.25
- targets: int32 [128], P('dp'), may hold values from 0 to 16383
- loss_weight: bfloat16 [128], P('dp'), may hold values from 2 to 20
- inputs: int32 [128], P('dp'), may hold values from 0 to 16383
- embed_grad: bfloat16 [128, 4608], P('dp'), may hold values from -0.09375 to 0.09375
Outputs:
- table_grad: bfloat16 [16384, 4608], P(('dp', 'tensor'))
- hidden_grad: float32 [128, 4608], P('dp', 'tensor')
All inputs are finite; a program needn't handle non-finite values.
Results may differ from a plain program's by a relative error of at most 0.0052.
Values may be sent and summed in bfloat16 or wider, within the bound.
A program may use at most 64 MiB of HBM per device.

v0:
```python
import math
import jax
import jax.numpy as jnp
from jax import lax
from jax.sharding import PartitionSpec as P


def squashed(hidden_rows, tied_table):
    logits = lax.dot_general(
        hidden_rows, tied_table, (((1,), (1,)), ((), ())), preferred_element_type=jnp.float32
    )
    return jnp.tanh(logits / 30.0)


def per_device(hidden, tied_table, targets, loss_weight, inputs, embed_grad):
    width = hidden.shape[1]
    vocab_rows = tied_table.shape[0]
    hidden_all, grad_all, target_all, weight_all, input_all = (
        lax.all_gather(hidden, "dp", axis=0, tiled=True),
        lax.all_gather(embed_grad, "dp", axis=0, tiled=True),
        lax.all_gather(targets, "dp", axis=0, tiled=True),
        lax.all_gather(loss_weight, "dp", axis=0, tiled=True),
        lax.all_gather(inputs, "dp", axis=0, tiled=True),
    )
    offset = lax.axis_index(("dp", "tensor")) * vocab_rows
    columns = offset + jnp.arange(vocab_rows)
    squash = squashed(hidden_all, tied_table)
    expo = jnp.exp(30.0 * squash)
    total = lax.psum(jnp.sum(expo, axis=1), ("dp", "tensor"))
    hits = (target_all[:, None] == columns[None, :]).astype(jnp.float32)
    weights = weight_all.astype(jnp.float32)
    dlogit = (weights[:, None] * (expo / total[:, None] - hits) * (1.0 - squash * squash)).astype(
        jnp.bfloat16
    )
    group_rows = lax.psum_scatter(
        jnp.dot(dlogit, tied_table, preferred_element_type=jnp.float32),
        "dp",
        scatter_dimension=0,
        tiled=True,
    )
    hidden_grad = lax.psum_scatter(group_rows, "tensor", scatter_dimension=1, tiled=True)
    head_term = lax.dot_general(
        dlogit, hidden_all, (((0,), (0,)), ((), ())), preferred_element_type=jnp.float32
    )
    onehot = (input_all[None, :] == columns[:, None]).astype(jnp.bfloat16)
    embed_term = jnp.dot(onehot, grad_all, preferred_element_type=jnp.float32)
    table_grad = (head_term + math.sqrt(width) * embed_term).astype(jnp.bfloat16)
    return (table_grad, hidden_grad)


def solution(mesh):
    placed = (P("dp", None), P(("dp", "tensor"), None), P("dp"), P("dp"), P("dp"), P("dp", None))
    return jax.shard_map(
        per_device,
        mesh=mesh,
        in_specs=placed,
        out_specs=(P(("dp", "tensor"), None), P("dp", "tensor")),
        check_vma=False,
    )
```

profile of v0, /device:TPU:0, one launch (start us, length us, event | category | flops | bytes accessed | tf_op | source)
XLA Modules:
  0.0 241.8 jit_solution(12632579317556245795)
XLA Ops:
  7.2 0.0 all-gather.3.cloned.1.call-start
  7.2 0.7 all-gather.3.cloned.1.call-update
  7.9 0.0 reduce-scatter.3.cloned.1.call-start
  8.0 1.2 dynamic-slice
  9.9 0.9 dynamic-update-slice
  10.7 23.2 %all-reduce = bf16[128]{0:T(256)(128)(2,1)S(1)} all-reduce(bf16[128]{0:T(256)(128)(2,1)S(1)} %dynamic-update-slice), channel_id=1, replica_groups=mesh['dp'=8,'tensor'=4] {'dp'}, use_global_device_ids=true, to_apply=%add | all-reduce | flops 128 | bytes 512
  34.0 0.9 dynamic-update-slice.1
  34.8 0.8 dynamic-update-slice.2
  35.7 6.8 %all-reduce.3 = (s32[128]{0:T(128)S(1)}, s32[128]{0:T(128)S(1)}) all-reduce(s32[128]{0:T(128)S(1)} %dynamic-update-slice.1, s32[128]{0:T(128)S(1)} %dynamic-update-slice.2), channel_id=1, replica_groups=mesh['dp'=8,'tensor'=4] {'dp'}, use_global_device_ids=true, to_apply=%add.1 | all-reduce | flops 256 | bytes 2048
  42.5 11.3 %all-gather.3.cloned.1.call-done = bf16[128,4608]{1,0:T(8,128)(2,1)} async-done(((bf16[16,4608]{1,0:T(8,128)(2,1)}), bf16[128,4608]{1,0:T(8,128)(2,1)}) %all-gather.3.cloned.1.call-update) | async-done | bytes 1179664 | tf_op jit(solution)/shard_map/all_gather | solution.py:19
  53.8 4.4 %fusion.1 = (f32[128]{0:T(128)S(1)}, f32[128,512]{1,0:T(8,128)S(1)}) fusion(bf16[128,4608]{1,0:T(8,128)(2,1)} %all-gather.3.cloned.1.call-done, bf16[512,4608]{1,0:T(8,128)(2,1)} %param.7), kind=kOutput, calls=%fused_computation.5 | convolution fusion | flops 604176256 | bytes 6160896 | tf_op jit(solution)/shard_map/dot_general | solution.py:9
  58.3 38.7 %psum.7 = f32[128]{0:T(128)S(1)} all-reduce(f32[128]{0:T(128)S(1)} %get-tuple-element.4), channel_id=1, replica_groups=mesh['dp'=8,'tensor'=4] {'dp','tensor'}, use_global_device_ids=true, to_apply=%region_1.0 | all-reduce | flops 128 | bytes 1024 | tf_op jit(solution)/shard_map/psum | solution.py:29
  96.9 0.0 copy-start
  96.9 4.7 %fusion.5 = f32[128,4608]{1,0:T(8,128)} fusion(bf16[512,4608]{1,0:T(8,128)(2,1)} %param.7, f32[128,512]{1,0:T(8,128)S(1)} %get-tuple-element.5, s32[512]{0:T(512)S(1)} %iota_add_fusion, f32[128]{0:T(128)S(1)} %psum.7, f32[128]{0:T(128)S(1)} %convert_element_type.13, s32[128]{0:T(128)S(1)} %get-tuple-element.2), kind=kOutput, calls=%fused_computation.10 | convolution fusion | flops 604635136 | bytes 7343616 | tf_op jit(solution)/shard_map/dot_general | solution.py:36
  101.6 0.0 reduce-scatter.3.cloned.1.call-update
  101.7 0.0 all-gather.5.cloned.1.call-start
  101.7 0.7 all-gather.5.cloned.1.call-update
  102.4 0.0 reduce-scatter.5.cloned.1.call-start
  102.5 0.0 copy-done
  102.5 5.2 %fusion.6 = f32[512,4608]{1,0:T(8,128)} fusion(bf16[128,4608]{1,0:T(8,128)(2,1)S(1)} %copy-done, f32[128,512]{1,0:T(8,128)S(1)} %get-tuple-element.5, s32[512]{0:T(512)S(1)} %iota_add_fusion, f32[128]{0:T(128)S(1)} %psum.7, f32[128]{0:T(128)S(1)} %convert_element_type.13, s32[128]{0:T(128)S(1)} %get-tuple-element.2), kind=kOutput, calls=%fused_computation.11 | convolution fusion | flops 604635136 | bytes 10882560 | tf_op jit(solution)/shard_map/dot_general | solution.py:42
  107.6 63.3 %reduce-scatter.3.cloned.1.call-done = f32[16,4608]{1,0:T(8,128)} async-done(((f32[128,4608]{1,0:T(8,128)}), f32[16,4608]{1,0:T(8,128)}) %reduce-scatter.3.cloned.1.call-update) | async-done | bytes 294928 | tf_op jit(solution)/shard_map/reduce_scatter | solution.py:35
  171.0 0.0 reduce-scatter.5.cloned.1.call-update
  171.0 42.3 %all-gather.5.cloned.1.call-done = bf16[128,4608]{1,0:T(8,128)(2,1)} async-done(((bf16[16,4608]{1,0:T(8,128)(2,1)}), bf16[128,4608]{1,0:T(8,128)(2,1)}) %all-gather.5.cloned.1.call-update) | async-done | bytes 1179664 | tf_op jit(solution)/shard_map/all_gather | solution.py:20
  213.3 7.7 %add_convert_fusion = bf16[512,4608]{1,0:T(8,128)(2,1)} fusion(f32[512,4608]{1,0:T(8,128)} %fusion.6, bf16[128,4608]{1,0:T(8,128)(2,1)} %all-gather.5.cloned.1.call-done, s32[128]{0:T(128)S(1)} %get-tuple-element.3, s32[512]{0:T(512)S(1)} %iota_add_fusion), kind=kOutput, calls=%fused_computation | convolution fusion | flops 611123200 | bytes 15337984 | tf_op jit(solution)/shard_map/dot_general | solution.py:46
  220.9 14.3 %reduce-scatter.5.cloned.1.call-done = f32[16,1152]{1,0:T(8,128)} async-done(((f32[16,4608]{1,0:T(8,128)}), f32[16,1152]{1,0:T(8,128)}) %reduce-scatter.5.cloned.1.call-update) | async-done | bytes 73744 | tf_op jit(solution)/shard_map/reduce_scatter | solution.py:41
  (5 shorter events, 0.0 us)
Async XLA Ops:
  7.2 46.7 %all-gather.3.cloned.1.call-start = ((), (), s32[]{:S(2)}) async-start(), calls=%async_computation.2 | async-start | bytes 1327104 | tf_op jit(solution)/shard_map/all_gather | solution.py:19
  7.9 163.1 %reduce-scatter.3.cloned.1.call-start = ((), (), s32[]{:S(2)}) async-start(), calls=%async_computation.4 | async-start | bytes 2654208 | tf_op jit(solution)/shard_map/reduce_scatter | solution.py:35
  96.9 5.5 %copy-start = (bf16[128,4608]{1,0:T(8,128)(2,1)S(1)}, bf16[128,4608]{1,0:T(8,128)(2,1)}, u32[]{:S(2)}) copy-start(bf16[128,4608]{1,0:T(8,128)(2,1)} %all-gather.3.cloned.1.call-done) | copy-start | bytes 3538948
  101.7 111.6 %all-gather.5.cloned.1.call-start = ((), (), s32[]{:S(2)}) async-start(), calls=%async_computation.3 | async-start | bytes 1327104 | tf_op jit(solution)/shard_map/all_gather | solution.py:20
  102.4 132.9 %reduce-scatter.5.cloned.1.call-start = ((), (), s32[]{:S(2)}) async-start(), calls=%async_computation.5 | async-start | bytes 368640 | tf_op jit(solution)/shard_map/reduce_scatter | solution.py:41
Sparse Core Ops, SparseCore 0:
  10.2 43.6 all-gather.2
  101.8 69.1 reduce-scatter.2
  173.1 40.0 all-gather.4
  216.2 19.0 reduce-scatter.4
where the time goes:
time: 242 us
  waiting for transfers between devices  133 us (55%)
  blocking collectives  68.7 us (28%)
  matrix products  22 us (9%)
  between operations  14.5 us (6%)
  local copies, waits for them, and re-layouts  3.81 us (2%)
    reduce_scatter x1, waiting for transfers between devices, per_device(): lax.psum_scatter(jnp.dot(dlogit, tied_table, preferred_element_type=jnp.f...  63.3 us
    all_gather x1, waiting for transfers between devices, per_device(): lax.all_gather(embed_grad, 'dp', axis=0, tiled=True)  42.3 us
    psum x1, blocking collectives, per_device(): total = lax.psum(jnp.sum(expo, axis=1), ('dp', 'tensor'))  38.7 us
    unnamed x2, blocking collectives  30.1 us
    reduce_scatter x1, waiting for transfers between devices, per_device(): lax.psum_scatter(group_rows, 'tensor', scatter_dimension=1, tiled=True)  14.3 us
    all_gather x1, waiting for transfers between devices, per_device(): lax.all_gather(hidden, 'dp', axis=0, tiled=True)  11.3 us
    dot_general x1, matrix products, per_device(): embed_term = jnp.dot(onehot, grad_all, preferred_element_type=jnp.float32)  7.67 us
    dot_general x1, matrix products, per_device(): lax.dot_general(dlogit, hidden_all, (((0,), (0,)), ((), ())), preferred_e...  5.16 us
  transfers between devices with their start and end apart: 4, of which 4 were waited for; matrix products, arithmetic and copies ran while one was open for 7% of the time, Pallas kernels for 0%

commit v1 on v0

--- a/solution.py
+++ b/solution.py
@@ -26,7 +26,8 @@
     columns = offset + jnp.arange(vocab_rows)
     squash = squashed(hidden_all, tied_table)
     expo = jnp.exp(30.0 * squash)
-    total = lax.psum(jnp.sum(expo, axis=1), ("dp", "tensor"))
+    one_axis = lax.psum(jnp.sum(expo, axis=1), "tensor")
+    total = lax.psum(one_axis, "dp")
     hits = (target_all[:, None] == columns[None, :]).astype(jnp.float32)
     weights = weight_all.astype(jnp.float32)
     dlogit = (weights[:, None] * (expo / total[:, None] - hits) * (1.0 - squash * squash)).astype(

time: 242 us -> 226 us (0.934)
  blocking collectives: 68.7 us -> 54.9 us
  waiting for transfers between devices: 133 us -> 130 us
    psum x1 -> x2, blocking collectives: 38.7 us -> 24.8 us  [the longest x1 19.2 us: per_device(): total = lax.psum(one_axis, 'dp')]
    reduce_scatter x1, waiting for transfers between devices: 63.3 us -> 60.7 us  [per_device(): lax.psum_scatter(jnp.dot(dlogit, tied_table, preferred_element_type=jnp.f...]
where the time goes in v1:
time: 226 us; the launch traced here: 225 us
  waiting for transfers between devices  130 us (58%)
  blocking collectives  54.9 us (24%)
  matrix products  22 us (10%)
  between operations  14.5 us (6%)
  local copies, waits for them, and re-layouts  3.81 us (2%)
    reduce_scatter x1, waiting for transfers between devices, per_device(): lax.psum_scatter(jnp.dot(dlogit, tied_table, preferred_element_type=jnp.f...  60.7 us
    all_gather x1, waiting for transfers between devices, per_device(): lax.all_gather(embed_grad, 'dp', axis=0, tiled=True)  42.3 us
    unnamed x2, blocking collectives  30.1 us
    psum x1, blocking collectives, per_device(): total = lax.psum(one_axis, 'dp')  19.2 us
    reduce_scatter x1, waiting for transfers between devices, per_device(): lax.psum_scatter(group_rows, 'tensor', scatter_dimension=1, tiled=True)  14.3 us
    all_gather x1, waiting for transfers between devices, per_device(): lax.all_gather(hidden, 'dp', axis=0, tiled=True)  11.3 us
    dot_general x1, matrix products, per_device(): embed_term = jnp.dot(onehot, grad_all, preferred_element_type=jnp.float32)  7.67 us
    psum x1, blocking collectives, per_device(): one_axis = lax.psum(jnp.sum(expo, axis=1), 'tensor')  5.67 us
  transfers between devices with their start and end apart: 4, of which 4 were waited for; matrix products, arithmetic and copies ran while one was open for 7% of the time, Pallas kernels for 0%

profile of v1, /device:TPU:0, one launch (start us, length us, event | category | flops | bytes accessed | tf_op | source)
XLA Modules:
  0.0 225.4 jit_solution(15398550447409349801)
XLA Ops:
  7.2 0.0 all-gather.3.cloned.1.call-start
  7.2 0.7 all-gather.3.cloned.1.call-update
  7.9 0.0 reduce-scatter.3.cloned.1.call-start
  8.0 1.2 dynamic-slice
  9.9 0.9 dynamic-update-slice
  10.7 23.2 %all-reduce = bf16[128]{0:T(256)(128)(2,1)S(1)} all-reduce(bf16[128]{0:T(256)(128)(2,1)S(1)} %dynamic-update-slice), channel_id=1, replica_groups=mesh['dp'=8,'tensor'=4] {'dp'}, use_global_device_ids=true, to_apply=%add | all-reduce | flops 128 | bytes 512
  34.0 0.9 dynamic-update-slice.1
  34.8 0.8 dynamic-update-slice.2
  35.7 6.8 %all-reduce.3 = (s32[128]{0:T(128)S(1)}, s32[128]{0:T(128)S(1)}) all-reduce(s32[128]{0:T(128)S(1)} %dynamic-update-slice.1, s32[128]{0:T(128)S(1)} %dynamic-update-slice.2), channel_id=1, replica_groups=mesh['dp'=8,'tensor'=4] {'dp'}, use_global_device_ids=true, to_apply=%add.1 | all-reduce | flops 256 | bytes 2048
  42.5 11.3 %all-gather.3.cloned.1.call-done = bf16[128,4608]{1,0:T(8,128)(2,1)} async-done(((bf16[16,4608]{1,0:T(8,128)(2,1)}), bf16[128,4608]{1,0:T(8,128)(2,1)}) %all-gather.3.cloned.1.call-update) | async-done | bytes 1179664 | tf_op jit(solution)/shard_map/all_gather | solution.py:19
  53.8 4.4 %fusion.1 = (f32[128]{0:T(128)S(1)}, f32[128,512]{1,0:T(8,128)S(1)}) fusion(bf16[128,4608]{1,0:T(8,128)(2,1)} %all-gather.3.cloned.1.call-done, bf16[512,4608]{1,0:T(8,128)(2,1)} %param.7), kind=kOutput, calls=%fused_computation.5 | convolution fusion | flops 604176256 | bytes 6160896 | tf_op jit(solution)/shard_map/dot_general | solution.py:9
  58.3 5.7 %psum.14 = f32[128]{0:T(128)S(1)} all-reduce(f32[128]{0:T(128)S(1)} %get-tuple-element.4), channel_id=1, replica_groups=mesh['dp'=8,'tensor'=4] {'tensor'}, use_global_device_ids=true, to_apply=%region_1.0 | all-reduce | flops 128 | bytes 1024 | tf_op jit(solution)/shard_map/psum | solution.py:29
  64.0 19.2 %psum.15 = f32[128]{0:T(128)S(1)} all-reduce(f32[128]{0:T(128)S(1)} %psum.14), channel_id=1, replica_groups=mesh['dp'=8,'tensor'=4] {'dp'}, use_global_device_ids=true, to_apply=%region_2.0 | all-reduce | flops 128 | bytes 1024 | tf_op jit(solution)/shard_map/psum | solution.py:30
  83.1 0.0 copy-start
  83.1 4.7 %fusion.5 = f32[128,4608]{1,0:T(8,128)} fusion(bf16[512,4608]{1,0:T(8,128)(2,1)} %param.7, f32[128,512]{1,0:T(8,128)S(1)} %get-tuple-element.5, s32[512]{0:T(512)S(1)} %iota_add_fusion, f32[128]{0:T(128)S(1)} %psum.15, f32[128]{0:T(128)S(1)} %convert_element_type.13, s32[128]{0:T(128)S(1)} %get-tuple-element.2), kind=kOutput, calls=%fused_computation.10 | convolution fusion | flops 604635136 | bytes 7343616 | tf_op jit(solution)/shard_map/dot_general | solution.py:37
  87.8 0.0 reduce-scatter.3.cloned.1.call-update
  87.9 0.0 all-gather.5.cloned.1.call-start
  87.9 0.7 all-gather.5.cloned.1.call-update
  88.6 0.0 reduce-scatter.5.cloned.1.call-start
  88.7 0.0 copy-done
  88.7 5.2 %fusion.6 = f32[512,4608]{1,0:T(8,128)} fusion(bf16[128,4608]{1,0:T(8,128)(2,1)S(1)} %copy-done, f32[128,512]{1,0:T(8,128)S(1)} %get-tuple-element.5, s32[512]{0:T(512)S(1)} %iota_add_fusion, f32[128]{0:T(128)S(1)} %psum.15, f32[128]{0:T(128)S(1)} %convert_element_type.13, s32[128]{0:T(128)S(1)} %get-tuple-element.2), kind=kOutput, calls=%fused_computation.11 | convolution fusion | flops 604635136 | bytes 10882560 | tf_op jit(solution)/shard_map/dot_general | solution.py:43
  93.8 60.7 %reduce-scatter.3.cloned.1.call-done = f32[16,4608]{1,0:T(8,128)} async-done(((f32[128,4608]{1,0:T(8,128)}), f32[16,4608]{1,0:T(8,128)}) %reduce-scatter.3.cloned.1.call-update) | async-done | bytes 294928 | tf_op jit(solution)/shard_map/reduce_scatter | solution.py:36
  154.6 0.0 reduce-scatter.5.cloned.1.call-update
  154.6 42.3 %all-gather.5.cloned.1.call-done = bf16[128,4608]{1,0:T(8,128)(2,1)} async-done(((bf16[16,4608]{1,0:T(8,128)(2,1)}), bf16[128,4608]{1,0:T(8,128)(2,1)}) %all-gather.5.cloned.1.call-update) | async-done | bytes 1179664 | tf_op jit(solution)/shard_map/all_gather | solution.py:20
  196.9 7.7 %add_convert_fusion = bf16[512,4608]{1,0:T(8,128)(2,1)} fusion(f32[512,4608]{1,0:T(8,128)} %fusion.6, bf16[128,4608]{1,0:T(8,128)(2,1)} %all-gather.5.cloned.1.call-done, s32[128]{0:T(128)S(1)} %get-tuple-element.3, s32[512]{0:T(512)S(1)} %iota_add_fusion), kind=kOutput, calls=%fused_computation | convolution fusion | flops 611123200 | bytes 15337984 | tf_op jit(solution)/shard_map/dot_general | solution.py:47
  204.6 14.3 %reduce-scatter.5.cloned.1.call-done = f32[16,1152]{1,0:T(8,128)} async-done(((f32[16,4608]{1,0:T(8,128)}), f32[16,1152]{1,0:T(8,128)}) %reduce-scatter.5.cloned.1.call-update) | async-done | bytes 73744 | tf_op jit(solution)/shard_map/reduce_scatter | solution.py:42
  (5 shorter events, 0.0 us)
Async XLA Ops:
  7.2 46.7 %all-gather.3.cloned.1.call-start = ((), (), s32[]{:S(2)}) async-start(), calls=%async_computation.2 | async-start | bytes 1327104 | tf_op jit(solution)/shard_map/all_gather | solution.py:19
  7.9 146.7 %reduce-scatter.3.cloned.1.call-start = ((), (), s32[]{:S(2)}) async-start(), calls=%async_computation.4 | async-start | bytes 2654208 | tf_op jit(solution)/shard_map/reduce_scatter | solution.py:36
  83.1 5.5 %copy-start = (bf16[128,4608]{1,0:T(8,128)(2,1)S(1)}, bf16[128,4608]{1,0:T(8,128)(2,1)}, u32[]{:S(2)}) copy-start(bf16[128,4608]{1,0:T(8,128)(2,1)} %all-gather.3.cloned.1.call-done) | copy-start | bytes 3538948
  87.9 109.0 %all-gather.5.cloned.1.call-start = ((), (), s32[]{:S(2)}) async-start(), calls=%async_computation.3 | async-start | bytes 1327104 | tf_op jit(solution)/shard_map/all_gather | solution.py:20
  88.6 130.3 %reduce-scatter.5.cloned.1.call-start = ((), (), s32[]{:S(2)}) async-start(), calls=%async_computation.5 | async-start | bytes 368640 | tf_op jit(solution)/shard_map/reduce_scatter | solution.py:42
Sparse Core Ops, SparseCore 0:
  10.2 43.6 all-gather.2
  88.0 66.5 reduce-scatter.2
  156.7 40.1 all-gather.4
  199.8 19.0 reduce-scatter.4
